TPU v7x, 32 devices: a whole 2x2x4 slice. The times are simulated.
32 devices in a mesh: axial: 8 (over y, x, core), span: 4 (over z).
Axes of the slice: x: 2, y: 2, z: 4, core: 2. Of those that a mesh axis runs over, the one named last changes fastest.
Arguments:
- stiffness: float32 [64, 32, 128], P('axial', 'span'), may hold values from 0.2 to 5
- adjoint_rhs: float32 [3, 64, 32, 128], P(None, 'axial', 'span'), may hold values from -96 to 96
- surf_cell: int32 [8, 2048], P('axial', 'span'), may hold values from 0 to 8191
- surf_live: int32 [8, 2048], P('axial', 'span'), may hold values from 0 to 1, as said below
- ffd_index: int32 [8, 8, 2048], P(None, 'axial', 'span'), may hold values from 0 to 4095, as said below
- ffd_weight: float32 [8, 8, 2048], P(None, 'axial', 'span'), may hold values from 0.03 to 0.3
- surf_direct: float32 [3, 8, 2048], P(None, 'axial', 'span'), may hold values from -6 to 6
- surf_metric: float32 [3, 8, 2048], P(None, 'axial', 'span'), may hold values from -6 to 6
Outputs:
- adjoint: float32 [3, 64, 32, 128], P(None, 'axial', 'span')
- ffd_grad: float32 [4096, 3], P(('axial', 'span'))
Inputs may be any that keep to these rules, and one draw needn't show every extreme that they name: `surf_live`: some device has all 512 of its slots live in every draw; the share of live slots differs from device to device. `ffd_index`: for the device at axial index u and span index t, with f = u times the span axis's size plus t and P = f plus half the number of devices, every control point named by its slots is (f - 1) * 128 + r or (P - 1) * 128 + r modulo 4096, for some r from 0 to 383.
All inputs are finite; a program needn't handle non-finite values.
Results may differ from a plain program's by a relative error of at most 0.000076.
Values sent between devices are 32-bit elements; how exact they have to be, the bound alone decides.
A program may use at most 64 MiB of HBM per device.

v0:
```python
import jax
import jax.numpy as jnp
from jax import lax
from jax.sharding import PartitionSpec as P

SWEEPS = 3
NFFD = 4096


neighbor_offsets = [
    (step_x, step_y, step_z)
    for step_x in (-1, 0, 1)
    for step_y in (-1, 0, 1)
    for step_z in (-1, 0, 1)
    if (step_x, step_y, step_z) != (0, 0, 0)
]


def extended(array, sides, width):
    for axis, dim in sides:
        count, length = (lax.axis_size(axis), array.shape[dim])
        up = [(i, (i + 1) % count) for i in range(count - 1)]
        down = [(j, i) for i, j in up]
        last = lax.slice_in_dim(array, length - width, length, axis=dim)
        first = lax.slice_in_dim(array, 0, width, axis=dim)
        before = lax.ppermute(last, axis, up)
        after = lax.ppermute(first, axis, down)
        array = jnp.concatenate([before, array, after], axis=dim)
    return array


def weight_of(offset):
    distance = abs(offset[0]) + abs(offset[1]) + abs(offset[2])
    return ({1: 1.0, 2: 0.5, 3: 0.25}[distance], distance)


def neighbor(values, step_x, step_y, step_z):
    row_count = values.shape[-3] - 2
    col_count = values.shape[-2] - 2
    window = values[
        ..., 1 + step_x : 1 + step_x + row_count, 1 + step_y : 1 + step_y + col_count, :
    ]
    if step_z != 0:
        window = jnp.roll(window, -step_z, axis=-1)
    return window


def diagonal_of(stiff_pad):
    summed = None
    for offset in neighbor_offsets:
        weight, distance = weight_of(offset)
        factor = 1.25 * weight + (0.25 if distance == 2 else 0.0)
        contribution = factor * neighbor(stiff_pad, *offset)
        summed = contribution if summed is None else summed + contribution
    return summed


def apply_operator(adjoint_pad, stiff_pad, diagonal):
    center = adjoint_pad[:, 1:-1, 1:-1, :]
    result = [diagonal * center[0], diagonal * center[1], diagonal * center[2]]
    for offset in neighbor_offsets:
        weight, distance = weight_of(offset)
        weighted = neighbor(stiff_pad, *offset)[None] * neighbor(adjoint_pad, *offset)
        for component in range(3):
            result[component] = result[component] - weight * weighted[component]
        if distance == 2:
            dims = [axis_pos for axis_pos in range(3) if offset[axis_pos] != 0]
            first_dim, second_dim = (dims[0], dims[1])
            parity = 0.25 * offset[first_dim] * offset[second_dim]
            result[first_dim] = result[first_dim] - parity * weighted[second_dim]
            result[second_dim] = result[second_dim] - parity * weighted[first_dim]
    return jnp.stack(result)


def local(
    stiffness, adjoint_rhs, surf_cell, surf_live, ffd_index, ffd_weight, surf_direct, surf_metric
):
    size_x, size_y, size_z = stiffness.shape
    stiff_pad = extended(stiffness, (("axial", 0), ("span", 1)), 1)
    diagonal = diagonal_of(stiff_pad)
    adjoint = adjoint_rhs / diagonal
    for iteration in range(SWEEPS):
        adjoint_pad = extended(adjoint, (("axial", 1), ("span", 2)), 1)
        adjoint = (
            adjoint + (adjoint_rhs - apply_operator(adjoint_pad, stiff_pad, diagonal)) / diagonal
        )
    flat_fields = adjoint.reshape(3, size_x * size_y * size_z)
    adjoint_at = jnp.take(flat_fields, surf_cell[0], axis=1)
    sensitivity = surf_live[0].astype(jnp.float32) * (
        surf_direct[:, 0] - surf_metric[:, 0] * adjoint_at
    )
    point_index = ffd_index[:, 0]
    point_weight = ffd_weight[:, 0]

    def block_rows(points):
        onehot_table = jnp.zeros((points.shape[0], point_index.shape[1]), jnp.float32)
        for entry in range(point_index.shape[0]):
            onehot_table = onehot_table + jnp.where(
                point_index[entry][None, :] == points[:, None], point_weight[entry][None, :], 0.0
            )
        return lax.dot_general(
            onehot_table,
            sensitivity,
            (((1,), (1,)), ((), ())),
            precision=lax.Precision.HIGHEST,
            preferred_element_type=jnp.float32,
        )

    device_count = lax.axis_size("axial") * lax.axis_size("span")
    owned = NFFD // device_count
    points = jnp.arange(owned * lax.axis_size(("axial", "span")), dtype=jnp.int32)
    row_total = points.shape[0]
    block_size = 128
    grouped = points.reshape(row_total // block_size, block_size)
    ffd_grad = lax.psum_scatter(
        lax.map(block_rows, grouped).reshape(row_total, 3),
        ("axial", "span"),
        scatter_dimension=0,
        tiled=True,
    )
    return (adjoint, ffd_grad)


def solution(mesh):
    return jax.shard_map(
        local,
        mesh=mesh,
        in_specs=(
            P("axial", "span", None),
            P(None, "axial", "span", None),
            P("axial", "span"),
            P("axial", "span"),
            P(None, "axial", "span"),
            P(None, "axial", "span"),
            P(None, "axial", "span"),
            P(None, "axial", "span"),
        ),
        out_specs=(P(None, "axial", "span", None), P(("axial", "span"), None)),
        check_vma=False,
    )
```

profile of v0, /device:TPU:0, one launch (start us, length us, event | category | flops | bytes accessed | tf_op | source)
XLA Modules:
  0.0 261.5 jit_solution(5895944465964179848)
XLA Ops:
  7.9 2.4 collective-permute-start
  10.3 1.3 collective-permute-start.1
  11.6 0.9 fusion.586
  12.5 0.9 fusion.587
  15.7 1.3 collective-permute-start.3
  17.1 4.5 %collective-permute-start.2 = (f32[10,1,128]{2,1,0:T(1,128)S(1)}, f32[10,1,128]{2,1,0:T(1,128)S(1)}, u32[]{:S(2)}, u32[]{:S(2)}) collective-permute-start(f32[10,1,128]{2,1,0:T(1,128)S(1)} %get-tuple-element.291), channel_id=1, source_target_pairs={{0,1},{1,2},{2,3},{4,5},{5,6},{6,7},{8,9},{9,10},{10,11},{12,13},{... | collective-permute-start | bytes 15368 | tf_op jit(solution)/shard_map/ppermute | solution.py:26
  21.9 1.1 collective-permute-done.2
  23.5 0.9 broadcast_divide_fusion
  24.4 3.4 %collective-permute-start.4 = (f32[3,1,8,128]{3,2,1,0:T(8,128)S(1)}, f32[3,1,8,128]{3,2,1,0:T(8,128)S(1)}, u32[]{:S(2)}, u32[]{:S(2)}) collective-permute-start(f32[3,1,8,128]{3,2,1,0:T(8,128)S(1)} %get-tuple-element.266), channel_id=1, source_target_pairs={{0,4},{4,8},{8,12},{12,16},{16,20},{20,24},{24,28},{1,5},{5,9},{9,... | collective-permute-start | bytes 36872 | tf_op jit(solution)/shard_map/ppermute | solution.py:26
  27.9 1.3 collective-permute-start.5
  29.2 4.1 %collective-permute-done.5 = f32[3,1,8,128]{3,2,1,0:T(8,128)S(1)} collective-permute-done((f32[3,1,8,128]{3,2,1,0:T(8,128)S(1)}, f32[3,1,8,128]{3,2,1,0:T(8,128)S(1)}, u32[]{:S(2)}, u32[]{:S(2)}) %collective-permute-start.5) | collective-permute-done | bytes 12320 | tf_op jit(solution)/shard_map/ppermute | solution.py:27
  33.3 4.2 %collective-permute-start.6 = (f32[3,10,1,128]{3,2,1,0:T(1,128)S(1)}, f32[3,10,1,128]{3,2,1,0:T(1,128)S(1)}, u32[]{:S(2)}, u32[]{:S(2)}) collective-permute-start(f32[3,10,1,128]{3,2,1,0:T(1,128)S(1)} %get-tuple-element.206), channel_id=1, source_target_pairs={{0,1},{1,2},{2,3},{4,5},{5,6},{6,7},{8,9},{9,10},{10,11},{12,13},{... | collective-permute-start | bytes 46088 | tf_op jit(solution)/shard_map/ppermute | solution.py:26
  37.5 1.3 collective-permute-start.7
  39.7 3.5 %collective-permute-done.7 = f32[3,10,1,128]{3,2,1,0:T(1,128)S(1)} collective-permute-done((f32[3,10,1,128]{3,2,1,0:T(1,128)S(1)}, f32[3,10,1,128]{3,2,1,0:T(1,128)S(1)}, u32[]{:S(2)}, u32[]{:S(2)}) %collective-permute-start.7) | collective-permute-done | bytes 15392 | tf_op jit(solution)/shard_map/ppermute | solution.py:27
  45.5 2.9 %collective-permute-start.8 = (f32[3,1,8,128]{3,2,1,0:T(8,128)S(1)}, f32[3,1,8,128]{3,2,1,0:T(8,128)S(1)}, u32[]{:S(2)}, u32[]{:S(2)}) collective-permute-start(f32[3,1,8,128]{3,2,1,0:T(8,128)S(1)} %get-tuple-element.254), channel_id=1, source_target_pairs={{0,4},{4,8},{8,12},{12,16},{16,20},{20,24},{24,28},{1,5},{5,9},{9,... | collective-permute-start | bytes 36872 | tf_op jit(solution)/shard_map/ppermute | solution.py:26
  48.4 1.3 collective-permute-start.9
  49.7 2.7 %collective-permute-done.9 = f32[3,1,8,128]{3,2,1,0:T(8,128)S(1)} collective-permute-done((f32[3,1,8,128]{3,2,1,0:T(8,128)S(1)}, f32[3,1,8,128]{3,2,1,0:T(8,128)S(1)}, u32[]{:S(2)}, u32[]{:S(2)}) %collective-permute-start.9) | collective-permute-done | bytes 12320 | tf_op jit(solution)/shard_map/ppermute | solution.py:27
  52.5 3.5 %collective-permute-start.10 = (f32[3,10,1,128]{3,2,1,0:T(1,128)S(1)}, f32[3,10,1,128]{3,2,1,0:T(1,128)S(1)}, u32[]{:S(2)}, u32[]{:S(2)}) collective-permute-start(f32[3,10,1,128]{3,2,1,0:T(1,128)S(1)} %get-tuple-element.202), channel_id=1, source_target_pairs={{0,1},{1,2},{2,3},{4,5},{5,6},{6,7},{8,9},{9,10},{10,11},{12,13},{... | collective-permute-start | bytes 46088 | tf_op jit(solution)/shard_map/ppermute | solution.py:26
  56.0 1.3 collective-permute-start.11
  58.1 3.5 %collective-permute-done.11 = f32[3,10,1,128]{3,2,1,0:T(1,128)S(1)} collective-permute-done((f32[3,10,1,128]{3,2,1,0:T(1,128)S(1)}, f32[3,10,1,128]{3,2,1,0:T(1,128)S(1)}, u32[]{:S(2)}, u32[]{:S(2)}) %collective-permute-start.11) | collective-permute-done | bytes 15392 | tf_op jit(solution)/shard_map/ppermute | solution.py:27
  64.0 3.1 %collective-permute-start.12 = (f32[3,1,8,128]{3,2,1,0:T(8,128)S(1)}, f32[3,1,8,128]{3,2,1,0:T(8,128)S(1)}, u32[]{:S(2)}, u32[]{:S(2)}) collective-permute-start(f32[3,1,8,128]{3,2,1,0:T(8,128)S(1)} %get-tuple-element.242), channel_id=1, source_target_pairs={{0,4},{4,8},{8,12},{12,16},{16,20},{20,24},{24,28},{1,5},{5,9},{9,... | collective-permute-start | bytes 36872 | tf_op jit(solution)/shard_map/ppermute | solution.py:26
  67.1 1.3 collective-permute-start.13
  68.8 3.0 %collective-permute-done.13 = f32[3,1,8,128]{3,2,1,0:T(8,128)S(1)} collective-permute-done((f32[3,1,8,128]{3,2,1,0:T(8,128)S(1)}, f32[3,1,8,128]{3,2,1,0:T(8,128)S(1)}, u32[]{:S(2)}, u32[]{:S(2)}) %collective-permute-start.13) | collective-permute-done | bytes 12320 | tf_op jit(solution)/shard_map/ppermute | solution.py:27
  71.9 3.5 %collective-permute-start.14 = (f32[3,10,1,128]{3,2,1,0:T(1,128)S(1)}, f32[3,10,1,128]{3,2,1,0:T(1,128)S(1)}, u32[]{:S(2)}, u32[]{:S(2)}) collective-permute-start(f32[3,10,1,128]{3,2,1,0:T(1,128)S(1)} %get-tuple-element.198), channel_id=1, source_target_pairs={{0,1},{1,2},{2,3},{4,5},{5,6},{6,7},{8,9},{9,10},{10,11},{12,13},{... | collective-permute-start | bytes 46088 | tf_op jit(solution)/shard_map/ppermute | solution.py:26
  75.3 1.3 collective-permute-start.15
  77.1 3.9 %collective-permute-done.15 = f32[3,10,1,128]{3,2,1,0:T(1,128)S(1)} collective-permute-done((f32[3,10,1,128]{3,2,1,0:T(1,128)S(1)}, f32[3,10,1,128]{3,2,1,0:T(1,128)S(1)}, u32[]{:S(2)}, u32[]{:S(2)}) %collective-permute-start.15) | collective-permute-done | bytes 15392 | tf_op jit(solution)/shard_map/ppermute | solution.py:27
  83.1 2.7 %copy.22 = f32[3,8,8,128]{0,3,2,1:T(8,128)} copy(f32[3,8,8,128]{3,2,1,0:T(8,128)S(1)} %fusion.93) | data formatting | bytes 196608 | tf_op jit(solution)/shard_map/add | solution.py:85
  85.8 3.2 %gather_fusion = f32[512,3]{1,0:T(8,128)S(1)} fusion(f32[3,8192]{0,1:T(8,128)} %bitcast.1705, s32[1024]{0:T(1024)S(1)} %pad_clamp_fusion), kind=kCustom, calls=%fused_computation | custom fusion | bytes 14336 | tf_op jit(solution)/shard_map/jit(_take)/gather | solution.py:88
  89.3 20.8 %while.10 = (s32[]{:T(128)}, f32[32,128,3]{1,2,0:T(4,128)S(1)}, s32[8,512]{1,0:T(8,128)S(1)}, s32[32,128]{1,0:T(8,128)S(1)}, f32[8,512]{1,0:T(8,128)S(1)}, /*index=5*/f32[3,512]{1,0:T(4,128)S(1)}, s32[]{:T(128)}) while((s32[]{:T(128)}, f32[32,128,3]{1,2,0:T(4,128)S(1)}, s32[8,512]{1,0:T(8,128)S(1)}, s32[32,128]{1,0:T(8,128)S(1)}, ...), condition=%wide.region_1.2_spmd, body=%wide.region_0.1_spmd.sunk | while | flops 3866626 | bytes 110165 | solution.py:116
  110.1 2.0 copy.25
  112.2 141.0 %reduce-scatter.4.cloned.1.call-done = f32[128,3]{1,0:T(8,128)} async-done(((f32[4096,3]{1,0:T(8,128)}), f32[128,3]{1,0:T(8,128)}) %reduce-scatter.4.cloned.1.call-update) | async-done | bytes 1552
  253.1 1.5 copy.26
  (270 shorter events, 32.9 us)
Async XLA Ops:
  7.2 22.0 %copy-start.4 = (s32[1,512]{1,0:T(1,128)S(1)}, s32[1,512]{1,0:T(1,128)}, u32[]{:S(2)}) copy-start(s32[1,512]{1,0:T(1,128)} %param.12) | copy-start | bytes 6148
  7.2 246.0 %reduce-scatter.4.cloned.1.call-start = ((), (), s32[]{:S(2)}) async-start(), calls=%async_computation.1 | async-start | bytes 2162688
  7.9 6.2 %collective-permute-start = (f32[1,8,128]{2,1,0:T(8,128)S(1)}, f32[1,8,128]{2,1,0:T(8,128)S(1)}, u32[]{:S(2)}, u32[]{:S(2)}) collective-permute-start(f32[1,8,128]{2,1,0:T(8,128)S(1)} %get-tuple-element.307), channel_id=1, source_target_pairs={{0,4},{4,8},{8,12},{12,16},{16,20},{20,24},{24,28},{1,5},{5,9},{9,... | collective-permute-start | bytes 12296 | tf_op jit(solution)/shard_map/ppermute | solution.py:26
  10.3 5.2 %collective-permute-start.1 = (f32[1,8,128]{2,1,0:T(8,128)S(1)}, f32[1,8,128]{2,1,0:T(8,128)S(1)}, u32[]{:S(2)}, u32[]{:S(2)}) collective-permute-start(f32[1,8,128]{2,1,0:T(8,128)S(1)} %get-tuple-element.308), channel_id=1, source_target_pairs={{4,0},{8,4},{12,8},{16,12},{20,16},{24,20},{28,24},{5,1},{9,5},{13... | collective-permute-start | bytes 12296 | tf_op jit(solution)/shard_map/ppermute | solution.py:27
  15.7 6.0 %collective-permute-start.3 = (f32[10,1,128]{2,1,0:T(1,128)S(1)}, f32[10,1,128]{2,1,0:T(1,128)S(1)}, u32[]{:S(2)}, u32[]{:S(2)}) collective-permute-start(f32[10,1,128]{2,1,0:T(1,128)S(1)} %get-tuple-element.290), channel_id=1, source_target_pairs={{1,0},{2,1},{3,2},{5,4},{6,5},{7,6},{9,8},{10,9},{11,10},{13,12},{... | collective-permute-start | bytes 15368 | tf_op jit(solution)/shard_map/ppermute | solution.py:27
  17.1 5.9 %collective-permute-start.2 = (f32[10,1,128]{2,1,0:T(1,128)S(1)}, f32[10,1,128]{2,1,0:T(1,128)S(1)}, u32[]{:S(2)}, u32[]{:S(2)}) collective-permute-start(f32[10,1,128]{2,1,0:T(1,128)S(1)} %get-tuple-element.291), channel_id=1, source_target_pairs={{0,1},{1,2},{2,3},{4,5},{5,6},{6,7},{8,9},{9,10},{10,11},{12,13},{... | collective-permute-start | bytes 15368 | tf_op jit(solution)/shard_map/ppermute | solution.py:26
  24.4 4.8 %collective-permute-start.4 = (f32[3,1,8,128]{3,2,1,0:T(8,128)S(1)}, f32[3,1,8,128]{3,2,1,0:T(8,128)S(1)}, u32[]{:S(2)}, u32[]{:S(2)}) collective-permute-start(f32[3,1,8,128]{3,2,1,0:T(8,128)S(1)} %get-tuple-element.266), channel_id=1, source_target_pairs={{0,4},{4,8},{8,12},{12,16},{16,20},{20,24},{24,28},{1,5},{5,9},{9,... | collective-permute-start | bytes 36872 | tf_op jit(solution)/shard_map/ppermute | solution.py:26
  27.9 5.4 %collective-permute-start.5 = (f32[3,1,8,128]{3,2,1,0:T(8,128)S(1)}, f32[3,1,8,128]{3,2,1,0:T(8,128)S(1)}, u32[]{:S(2)}, u32[]{:S(2)}) collective-permute-start(f32[3,1,8,128]{3,2,1,0:T(8,128)S(1)} %get-tuple-element.267), channel_id=1, source_target_pairs={{4,0},{8,4},{12,8},{16,12},{20,16},{24,20},{28,24},{5,1},{9,5},{13... | collective-permute-start | bytes 36872 | tf_op jit(solution)/shard_map/ppermute | solution.py:27
  33.3 6.3 %collective-permute-start.6 = (f32[3,10,1,128]{3,2,1,0:T(1,128)S(1)}, f32[3,10,1,128]{3,2,1,0:T(1,128)S(1)}, u32[]{:S(2)}, u32[]{:S(2)}) collective-permute-start(f32[3,10,1,128]{3,2,1,0:T(1,128)S(1)} %get-tuple-element.206), channel_id=1, source_target_pairs={{0,1},{1,2},{2,3},{4,5},{5,6},{6,7},{8,9},{9,10},{10,11},{12,13},{... | collective-permute-start | bytes 46088 | tf_op jit(solution)/shard_map/ppermute | solution.py:26
  37.5 5.6 %collective-permute-start.7 = (f32[3,10,1,128]{3,2,1,0:T(1,128)S(1)}, f32[3,10,1,128]{3,2,1,0:T(1,128)S(1)}, u32[]{:S(2)}, u32[]{:S(2)}) collective-permute-start(f32[3,10,1,128]{3,2,1,0:T(1,128)S(1)} %get-tuple-element.207), channel_id=1, source_target_pairs={{1,0},{2,1},{3,2},{5,4},{6,5},{7,6},{9,8},{10,9},{11,10},{13,12},{... | collective-permute-start | bytes 46088 | tf_op jit(solution)/shard_map/ppermute | solution.py:27
  44.0 1.4 copy-start
  45.5 4.2 %collective-permute-start.8 = (f32[3,1,8,128]{3,2,1,0:T(8,128)S(1)}, f32[3,1,8,128]{3,2,1,0:T(8,128)S(1)}, u32[]{:S(2)}, u32[]{:S(2)}) collective-permute-start(f32[3,1,8,128]{3,2,1,0:T(8,128)S(1)} %get-tuple-element.254), channel_id=1, source_target_pairs={{0,4},{4,8},{8,12},{12,16},{16,20},{20,24},{24,28},{1,5},{5,9},{9,... | collective-permute-start | bytes 36872 | tf_op jit(solution)/shard_map/ppermute | solution.py:26
  48.4 4.1 %collective-permute-start.9 = (f32[3,1,8,128]{3,2,1,0:T(8,128)S(1)}, f32[3,1,8,128]{3,2,1,0:T(8,128)S(1)}, u32[]{:S(2)}, u32[]{:S(2)}) collective-permute-start(f32[3,1,8,128]{3,2,1,0:T(8,128)S(1)} %get-tuple-element.255), channel_id=1, source_target_pairs={{4,0},{8,4},{12,8},{16,12},{20,16},{24,20},{28,24},{5,1},{9,5},{13... | collective-permute-start | bytes 36872 | tf_op jit(solution)/shard_map/ppermute | solution.py:27
  52.5 5.6 %collective-permute-start.10 = (f32[3,10,1,128]{3,2,1,0:T(1,128)S(1)}, f32[3,10,1,128]{3,2,1,0:T(1,128)S(1)}, u32[]{:S(2)}, u32[]{:S(2)}) collective-permute-start(f32[3,10,1,128]{3,2,1,0:T(1,128)S(1)} %get-tuple-element.202), channel_id=1, source_target_pairs={{0,1},{1,2},{2,3},{4,5},{5,6},{6,7},{8,9},{9,10},{10,11},{12,13},{... | collective-permute-start | bytes 46088 | tf_op jit(solution)/shard_map/ppermute | solution.py:26
  56.0 5.6 %collective-permute-start.11 = (f32[3,10,1,128]{3,2,1,0:T(1,128)S(1)}, f32[3,10,1,128]{3,2,1,0:T(1,128)S(1)}, u32[]{:S(2)}, u32[]{:S(2)}) collective-permute-start(f32[3,10,1,128]{3,2,1,0:T(1,128)S(1)} %get-tuple-element.203), channel_id=1, source_target_pairs={{1,0},{2,1},{3,2},{5,4},{6,5},{7,6},{9,8},{10,9},{11,10},{13,12},{... | collective-permute-start | bytes 46088 | tf_op jit(solution)/shard_map/ppermute | solution.py:27
  62.3 6.1 %copy-start.5 = (f32[3,1,512]{2,1,0:T(1,128)S(1)}, f32[3,1,512]{2,1,0:T(1,128)}, u32[]{:S(2)}) copy-start(f32[3,1,512]{2,1,0:T(1,128)} %param.16) | copy-start | bytes 18436
  62.3 6.2 %copy-start.6 = (f32[3,1,512]{2,1,0:T(1,128)S(1)}, f32[3,1,512]{2,1,0:T(1,128)}, u32[]{:S(2)}) copy-start(f32[3,1,512]{2,1,0:T(1,128)} %param.17) | copy-start | bytes 18436
  62.4 6.3 %copy-start.7 = (s32[1,512]{1,0:T(1,128)S(1)}, s32[1,512]{1,0:T(1,128)}, u32[]{:S(2)}) copy-start(s32[1,512]{1,0:T(1,128)} %param.13) | copy-start | bytes 6148
  62.5 6.3 %copy-start.2 = (f32[8,1,512]{2,1,0:T(1,128)S(1)}, f32[8,1,512]{2,1,0:T(1,128)}, u32[]{:S(2)}) copy-start(f32[8,1,512]{2,1,0:T(1,128)} %param.15) | copy-start | bytes 49156
  62.5 6.3 %copy-start.3 = (s32[8,1,512]{2,1,0:T(1,128)S(1)}, s32[8,1,512]{2,1,0:T(1,128)}, u32[]{:S(2)}) copy-start(s32[8,1,512]{2,1,0:T(1,128)} %param.14) | copy-start | bytes 49156
  64.0 4.8 %collective-permute-start.12 = (f32[3,1,8,128]{3,2,1,0:T(8,128)S(1)}, f32[3,1,8,128]{3,2,1,0:T(8,128)S(1)}, u32[]{:S(2)}, u32[]{:S(2)}) collective-permute-start(f32[3,1,8,128]{3,2,1,0:T(8,128)S(1)} %get-tuple-element.242), channel_id=1, source_target_pairs={{0,4},{4,8},{8,12},{12,16},{16,20},{20,24},{24,28},{1,5},{5,9},{9,... | collective-permute-start | bytes 36872 | tf_op jit(solution)/shard_map/ppermute | solution.py:26
  67.1 4.8 %collective-permute-start.13 = (f32[3,1,8,128]{3,2,1,0:T(8,128)S(1)}, f32[3,1,8,128]{3,2,1,0:T(8,128)S(1)}, u32[]{:S(2)}, u32[]{:S(2)}) collective-permute-start(f32[3,1,8,128]{3,2,1,0:T(8,128)S(1)} %get-tuple-element.243), channel_id=1, source_target_pairs={{4,0},{8,4},{12,8},{16,12},{20,16},{24,20},{28,24},{5,1},{9,5},{13... | collective-permute-start | bytes 36872 | tf_op jit(solution)/shard_map/ppermute | solution.py:27
  71.9 5.2 %collective-permute-start.14 = (f32[3,10,1,128]{3,2,1,0:T(1,128)S(1)}, f32[3,10,1,128]{3,2,1,0:T(1,128)S(1)}, u32[]{:S(2)}, u32[]{:S(2)}) collective-permute-start(f32[3,10,1,128]{3,2,1,0:T(1,128)S(1)} %get-tuple-element.198), channel_id=1, source_target_pairs={{0,1},{1,2},{2,3},{4,5},{5,6},{6,7},{8,9},{9,10},{10,11},{12,13},{... | collective-permute-start | bytes 46088 | tf_op jit(solution)/shard_map/ppermute | solution.py:26
  75.3 5.6 %collective-permute-start.15 = (f32[3,10,1,128]{3,2,1,0:T(1,128)S(1)}, f32[3,10,1,128]{3,2,1,0:T(1,128)S(1)}, u32[]{:S(2)}, u32[]{:S(2)}) collective-permute-start(f32[3,10,1,128]{3,2,1,0:T(1,128)S(1)} %get-tuple-element.199), channel_id=1, source_target_pairs={{1,0},{2,1},{3,2},{5,4},{6,5},{7,6},{9,8},{10,9},{11,10},{13,12},{... | collective-permute-start | bytes 46088 | tf_op jit(solution)/shard_map/ppermute | solution.py:27
  83.1 6.2 %copy-start.1 = (f32[3,8,8,128]{3,2,1,0:T(8,128)}, f32[3,8,8,128]{3,2,1,0:T(8,128)S(1)}, u32[]{:S(2)}) copy-start(f32[3,8,8,128]{3,2,1,0:T(8,128)S(1)} %fusion.93) | copy-start | bytes 294916
Sparse Core Ops, SparseCore 0:
  112.3 140.8 reduce-scatter.3
where the time goes:
time: 262 us; the launch traced here: 261 us
  waiting for transfers between devices  163 us (62%)
  starting transfers between devices  37.9 us (14%)
  local copies, waits for them, and re-layouts  18.2 us (7%)
  matrix products  17.1 us (7%)
  between operations  15 us (6%)
  other arithmetic  9.16 us (3%)
    unnamed x2, waiting for transfers between devices  141 us
    ppermute x8, starting transfers between devices, extended(): before = lax.ppermute(last, axis, up)  27.5 us
    ppermute x8, waiting for transfers between devices, extended(): after = lax.ppermute(first, axis, down)  21.3 us
    dot_general x32, matrix products, block_rows(): lax.dot_general(onehot_table, sensitivity, (((1,), (1,)), ((), ())), prec...  17.1 us
    ppermute x8, starting transfers between devices, extended(): after = lax.ppermute(first, axis, down)  10.3 us
  transfers between devices with their start and end apart: 17, of which 9 were waited for; matrix products, arithmetic and copies ran while one was open for 2% of the time, Pallas kernels for 0%

commit v1 on v0

v1 whole, which is shorter than its diff:
```python
import functools

import jax
import jax.numpy as jnp
from jax import lax
from jax.experimental import pallas as pl
from jax.experimental.pallas import tpu as pltpu
from jax.sharding import PartitionSpec as P

SWEEPS = 3
NFFD = 4096
CHUNK = 2
MESH = pl.DeviceIdType.MESH
DIRS = [(dx, dy) for dx in (-1, 0, 1) for dy in (-1, 0, 1) if (dx, dy) != (0, 0)]


def yshift(a, step):
    return pltpu.roll(a, (-step) % 16, 1)


def zshift(a, step):
    return pltpu.roll(a, (-step) % 128, 2)


def chunks(lo, hi):
    return [(c, min(CHUNK, hi - c)) for c in range(lo, hi, CHUNK)]


def kernel(
    n_axial, n_span,
    stiff, rhs, cell, live, index, weight, direct, metric,
    adj_out, grad_out,
    s_ext, r_ext, inv_ref, v_ref, p_ref, q_ref, own_v,
    cell_v, live_v, index_v, weight_v, direct_v, metric_v,
    zhot, lohot, mw, send_g, recv_g, grad_v,
    halo_send, halo_recv, g_send, g_recv, local_sem,
):
    u = lax.axis_index("axial")
    t = lax.axis_index("span")
    count = n_axial * n_span
    owned = NFFD // count
    f = u * n_span + t
    lows = lohot.shape[1]

    loads = [
        pltpu.make_async_copy(stiff, s_ext.at[pl.ds(4, 8), pl.ds(0, 8)], local_sem.at[0]),
        pltpu.make_async_copy(rhs, r_ext.at[:, pl.ds(4, 8), pl.ds(0, 8)], local_sem.at[1]),
        pltpu.make_async_copy(cell, cell_v, local_sem.at[2]),
        pltpu.make_async_copy(live, live_v, local_sem.at[3]),
        pltpu.make_async_copy(index, index_v, local_sem.at[4]),
        pltpu.make_async_copy(weight, weight_v, local_sem.at[5]),
        pltpu.make_async_copy(direct, direct_v, local_sem.at[6]),
        pltpu.make_async_copy(metric, metric_v, local_sem.at[7]),
    ]
    for load in loads[2:]:
        load.start()

    zero = jnp.zeros((8, 8, 128), jnp.float32)
    zero4 = jnp.zeros((4, 16, 128), jnp.float32)
    s_ext[0:4] = zero4
    s_ext[12:16] = zero4
    s_ext[4:12, 8:16] = zero
    for i in range(3):
        r_ext[i, 0:4] = zero4
        r_ext[i, 12:16] = zero4
        r_ext[i, 4:12, 8:16] = zero
    loads[0].start()
    loads[1].start()

    def owner(h):
        base = f + (count - 1) + h if h < 3 else f + (count - 1) + count // 2 + (h - 3)
        d = lax.rem(base, count)
        return (lax.div(d, n_span), lax.rem(d, n_span))

    def sender(h):
        base = f + count + 1 - h if h < 3 else f + count // 2 + count + 1 - (h - 3)
        d = lax.rem(base, count)
        return (lax.div(d, n_span), lax.rem(d, n_span))

    def exists(dx, dy):
        ok = None
        for step, pos, size in ((dx, u, n_axial), (dy, t, n_span)):
            if step != 0:
                one = (pos + step >= 0) & (pos + step < size)
                ok = one if ok is None else ok & one
        return ok

    barrier = pltpu.get_barrier_semaphore()
    for dx, dy in DIRS:
        @pl.when(exists(dx, dy))
        def _(dx=dx, dy=dy):
            pl.semaphore_signal(barrier, inc=1, device_id=(u + dx, t + dy), device_id_type=MESH)
    for h in (0, 2, 3, 4, 5):
        pl.semaphore_signal(barrier, inc=1, device_id=sender(h), device_id_type=MESH)
    def span_of(pos, size):
        return 1 + (pos > 0).astype(jnp.int32) + (pos < size - 1).astype(jnp.int32)

    pl.semaphore_wait(barrier, span_of(u, n_axial) * span_of(t, n_span) + 4)

    def halo(k):
        dx, dy = DIRS[k]

        def xs(width):
            if dx == 1:
                return pl.ds(8 - width, width), pl.ds(4 - width, width)
            if dx == -1:
                return pl.ds(0, width), pl.ds(12, width)
            return pl.ds(0, 8), pl.ds(4, 8)

        ysrc, ydst = {1: (pl.ds(4, 4), pl.ds(12, 4)), -1: (pl.ds(0, 4), pl.ds(8, 4)), 0: (pl.ds(0, 8), pl.ds(0, 8))}[dy]
        sx, sxd = xs(4)
        rx, rxd = xs(3)
        target = (u + dx, t + dy)
        return (
            pltpu.make_async_remote_copy(
                stiff.at[sx, ysrc], s_ext.at[sxd, ydst], halo_send.at[k, 0], halo_recv.at[k, 0],
                device_id=target, device_id_type=MESH),
            pltpu.make_async_remote_copy(
                rhs.at[:, rx, ysrc], r_ext.at[:, rxd, ydst], halo_send.at[k, 1], halo_recv.at[k, 1],
                device_id=target, device_id_type=MESH),
        )

    for k, (dx, dy) in enumerate(DIRS):
        @pl.when(exists(dx, dy))
        def _(k=k):
            for copy in halo(k):
                copy.start()

    for load in loads[2:]:
        load.wait()
    cells = cell_v[...]
    slots = cells.shape[1]
    z_of = cells & 127
    row_of = lax.shift_right_logical(cells, 7)
    zhot[...] = jnp.where(
        lax.broadcasted_iota(jnp.int32, (128, slots), 0) == z_of, 1.0, 0.0
    ).astype(jnp.bfloat16)
    for e in range(8):
        r = (index_v[e] - (f - 1) * owned + 2 * NFFD) & (NFFD - 1)
        r = jnp.where(r >= NFFD // 2, r - NFFD // 2 + 3 * owned, r)
        hi = lax.shift_right_logical(r, owned.bit_length() - 1)
        low = r & (owned - 1)
        lohot[e] = jnp.where(
            lax.broadcasted_iota(jnp.int32, (lows, slots), 0) == low, 1.0, 0.0
        ).astype(jnp.bfloat16)
        mw[e] = jnp.where(
            lax.broadcasted_iota(jnp.int32, (8, slots), 0) == hi, weight_v[e], 0.0
        )
    loads[0].wait()
    loads[1].wait()

    for k, (dx, dy) in enumerate(DIRS):
        @pl.when(exists(-dx, -dy))
        def _(k=k):
            for copy in halo(k):
                copy.wait_recv()

    for c, n in chunks(0, 16):
        s = s_ext[c:c + n]
        sy = yshift(s, 1) + yshift(s, -1)
        sz = zshift(s, 1) + zshift(s, -1)
        syz = zshift(sy, 1) + zshift(sy, -1)
        p_ref[0, c:c + n] = 1.25 * s + 0.875 * (sy + sz) + 0.3125 * syz
        p_ref[1, c:c + n] = 1.25 * (sy + sz) + 0.875 * syz
    for c, n in chunks(1, 15):
        diag = p_ref[0, c - 1:c - 1 + n] + p_ref[0, c + 1:c + 1 + n] + p_ref[1, c:c + n]
        inv = jnp.where(s_ext[c:c + n] > 0, 1.0 / diag, 0.0)
        inv_ref[c:c + n] = inv
        q_ref[5, c:c + n] = diag
        for i in range(3):
            v_ref[i, c:c + n] = r_ext[i, c:c + n] * inv

    for sweep in range(SWEEPS):
        lo, hi = 2 + sweep, 14 - sweep
        for c, n in chunks(lo - 1, hi + 1):
            s = s_ext[c:c + n]
            ux, uy, uz = [s * v_ref[i, c:c + n] for i in range(3)]
            yp, ym = yshift(ux, 1), yshift(ux, -1)
            a = 2.0 * ux + (yp + ym)
            q_ref[1, c:c + n] = yp - ym
            p_ref[0, c:c + n] = 0.5 * a + 0.25 * (zshift(a, 1) + zshift(a, -1))
            q_ref[2, c:c + n] = zshift(ux, 1) - zshift(ux, -1)
            yp, ym = yshift(uy, 1), yshift(uy, -1)
            a = 2.0 * uy + (yp + ym)
            dy_uy = yp - ym
            p_ref[1, c:c + n] = 0.5 * a + 0.25 * (zshift(a, 1) + zshift(a, -1))
            q_ref[4, c:c + n] = zshift(dy_uy, 1) - zshift(dy_uy, -1)
            zp, zm = zshift(uz, 1), zshift(uz, -1)
            a = 2.0 * uz + (zp + zm)
            dz_uz = zp - zm
            p_ref[2, c:c + n] = 0.5 * a + 0.25 * (yshift(a, 1) + yshift(a, -1))
            q_ref[3, c:c + n] = yshift(dz_uz, 1) - yshift(dz_uz, -1)
            q_ref[0, c:c + n] = dy_uy + dz_uz
        for c, n in chunks(lo, hi):
            mid, up, down = slice(c, c + n), slice(c + 1, c + 1 + n), slice(c - 1, c - 1 + n)
            s = s_ext[mid]
            inv = inv_ref[mid]
            factor = q_ref[5, mid] + 2.0 * s
            cross = [
                q_ref[0, up] - q_ref[0, down],
                q_ref[1, up] - q_ref[1, down] + q_ref[3, mid],
                q_ref[2, up] - q_ref[2, down] + q_ref[4, mid],
            ]
            for i in range(3):
                v = v_ref[i, mid]
                smooth = p_ref[i, up] + p_ref[i, down] + 2.0 * p_ref[i, mid]
                av = factor * v - smooth - 0.25 * cross[i]
                new = v + (r_ext[i, mid] - av) * inv
                if sweep < SWEEPS - 1:
                    v_ref[i, mid] = new
                else:
                    own_v[i, c - 4:c - 4 + n] = new[:, 0:8]

    out = pltpu.make_async_copy(own_v, adj_out, local_sem.at[0])
    out.start()

    rows = own_v.shape[1] * own_v.shape[2]
    flat = own_v[...].reshape(3 * rows, 128)
    top = flat.astype(jnp.bfloat16)
    rest = (flat - top.astype(jnp.float32)).astype(jnp.bfloat16)
    at = jnp.dot(top, zhot[...], preferred_element_type=jnp.float32)
    at = at + jnp.dot(rest, zhot[...], preferred_element_type=jnp.float32)
    row_mask = lax.broadcasted_iota(jnp.int32, (rows, slots), 0) == row_of
    live_f = live_v[...].astype(jnp.float32)
    sens = []
    for i in range(3):
        picked = jnp.where(row_mask, at[i * rows:(i + 1) * rows], 0.0)
        adj_at = jnp.sum(picked, axis=0, keepdims=True)
        sens.append(live_f * (direct_v[i] - metric_v[i] * adj_at))
    total = jnp.zeros((48, lows), jnp.float32)
    for e in range(8):
        parts = jnp.concatenate([mw[e] * sens[i] for i in range(3)], axis=0)
        top = parts.astype(jnp.bfloat16).astype(jnp.float32)
        both = jnp.concatenate([top, parts - top], axis=0).astype(jnp.bfloat16)
        total = total + lax.dot_general(
            both, lohot[e], (((1,), (1,)), ((), ())), preferred_element_type=jnp.float32
        )
    total = total[0:24] + total[24:48]
    for h in range(6):
        for i in range(3):
            send_g[h, i:i + 1] = total[8 * i + h:8 * i + h + 1]

    sends = {
        h: pltpu.make_async_remote_copy(
            send_g.at[h], recv_g.at[h], g_send.at[h], g_recv.at[h],
            device_id=owner(h), device_id_type=MESH)
        for h in (0, 2, 3, 4, 5)
    }
    for copy in sends.values():
        copy.start()
    for k, (dx, dy) in enumerate(DIRS):
        @pl.when(exists(dx, dy))
        def _(k=k):
            for copy in halo(k):
                copy.wait_send()
    acc = send_g[1, 0:3]
    for h, copy in sends.items():
        copy.wait_recv()
        acc = acc + recv_g[h, 0:3]
    grad_v[...] = acc
    final = pltpu.make_async_copy(grad_v, grad_out, local_sem.at[1])
    final.start()
    for copy in sends.values():
        copy.wait_send()
    out.wait()
    final.wait()


def local(stiffness, adjoint_rhs, surf_cell, surf_live, ffd_index, ffd_weight, surf_direct, surf_metric):
    n_axial, n_span = lax.axis_size("axial"), lax.axis_size("span")
    owned = NFFD // (n_axial * n_span)
    lows = max(owned, 128)
    slots = surf_cell.shape[1]
    f32, i32 = jnp.float32, jnp.int32
    any_spec = pl.BlockSpec(memory_space=pl.ANY)
    dma = pltpu.SemaphoreType.DMA
    adjoint, grad = pl.pallas_call(
        functools.partial(kernel, n_axial, n_span),
        out_shape=(
            jax.ShapeDtypeStruct(adjoint_rhs.shape, f32),
            jax.ShapeDtypeStruct((3, lows), f32),
        ),
        in_specs=[any_spec] * 8,
        out_specs=(any_spec, any_spec),
        scratch_shapes=[
            pltpu.VMEM((16, 16, 128), f32),
            pltpu.VMEM((3, 16, 16, 128), f32),
            pltpu.VMEM((16, 16, 128), f32),
            pltpu.VMEM((3, 16, 16, 128), f32),
            pltpu.VMEM((3, 16, 16, 128), f32),
            pltpu.VMEM((6, 16, 16, 128), f32),
            pltpu.VMEM(adjoint_rhs.shape, f32),
            pltpu.VMEM(surf_cell.shape, i32),
            pltpu.VMEM(surf_live.shape, i32),
            pltpu.VMEM(ffd_index.shape, i32),
            pltpu.VMEM(ffd_weight.shape, f32),
            pltpu.VMEM(surf_direct.shape, f32),
            pltpu.VMEM(surf_metric.shape, f32),
            pltpu.VMEM((128, slots), jnp.bfloat16),
            pltpu.VMEM((8, lows, slots), jnp.bfloat16),
            pltpu.VMEM((8, 8, slots), f32),
            pltpu.VMEM((6, 8, lows), f32),
            pltpu.VMEM((6, 8, lows), f32),
            pltpu.VMEM((3, lows), f32),
            dma((8, 2)),
            dma((8, 2)),
            dma((6,)),
            dma((6,)),
            dma((8,)),
        ],
        compiler_params=pltpu.CompilerParams(collective_id=0, has_side_effects=True),
    )(stiffness, adjoint_rhs, surf_cell, surf_live, ffd_index, ffd_weight, surf_direct, surf_metric)
    return adjoint, grad[:, :owned].T


def solution(mesh):
    return jax.shard_map(
        local,
        mesh=mesh,
        in_specs=(
            P("axial", "span", None),
            P(None, "axial", "span", None),
            P("axial", "span"),
            P("axial", "span"),
            P(None, "axial", "span"),
            P(None, "axial", "span"),
            P(None, "axial", "span"),
            P(None, "axial", "span"),
        ),
        out_specs=(P(None, "axial", "span", None), P(("axial", "span"), None)),
        check_vma=False,
    )
```

time: 262 us -> 21 us (0.08)
  waiting for transfers between devices: 163 us -> 0 us
  starting transfers between devices: 37.9 us -> 0 us
  Pallas kernels: 0 us -> 18.1 us
  matrix products: 17.1 us -> 0 us
  local copies, waits for them, and re-layouts: 18.2 us -> 2.12 us
  between operations: 15 us -> 0.65 us
  other arithmetic: 9.16 us -> 0 us
    unnamed x2 -> x0, waiting for transfers between devices: 141 us -> none
    ppermute x16 -> x0, starting transfers between devices: 37.9 us -> none  [the longest x8 27.5 us: extended(): before = lax.ppermute(last, axis, up)]
    ppermute x16 -> x0, waiting for transfers between devices: 22.4 us -> none  [the longest x8 21.3 us: extended(): after = lax.ppermute(first, axis, down)]
    pallas_call x0 -> x1, Pallas kernels: none -> 18.1 us  [local(): pl.pallas_call(functools.partial(kernel, n_axial, n_span), out_shape=(jax...]
    dot_general x32 -> x0, matrix products: 17.1 us -> none  [block_rows(): lax.dot_general(onehot_table, sensitivity, (((1,), (1,)), ((), ())), prec...]
    slice x89 -> x0, local copies, waits for them, and re-layouts: 7.16 us -> none  [the longest x18 3.84 us: neighbor(): window = jnp.roll(window, -step_z, axis=-1)]
    mul x49 -> x0, other arithmetic: 4.66 us -> none  [the longest x48 4.46 us: apply_operator(): neighbor(stiff_pad, *offset)[None] * neighbor(adjoint_pad, *offset)]
    gather x1 -> x0, local copies, waits for them, and re-layouts: 3.22 us -> none  [local(): adjoint_at = jnp.take(flat_fields, surf_cell[0], axis=1)]
  transfers between devices with their start and end apart: 17 -> 0, of which waited for: 9 -> 0; matrix products, arithmetic and copies ran while one was open for 2% -> 0% of each run, Pallas kernels for 0% -> 0%
where the time goes in v1:
time: 21 us; the launch traced here: 20.9 us
  Pallas kernels  18.1 us (86%)
  local copies, waits for them, and re-layouts  2.12 us (10%)
  between operations  0.65 us (3%)
    pallas_call x1, Pallas kernels, local(): pl.pallas_call(functools.partial(kernel, n_axial, n_span), out_shape=(jax...  18.1 us
    unnamed x4, local copies, waits for them, and re-layouts  2.12 us

profile of v1, /device:TPU:0, one launch (start us, length us, event | category | flops | bytes accessed | tf_op | source)
XLA Modules:
  0.0 20.9 jit_solution(899520901501812763)
XLA Ops:
  0.6 18.1 %shard_map.95 = (f32[3,8,8,128]{3,2,1,0:T(8,128)}, f32[3,128]{1,0:T(4,128)}) custom-call(f32[8,8,128]{2,1,0:T(8,128)} %stiff.1, f32[3,8,8,128]{3,2,1,0:T(8,128)} %rhs.1, s32[1,512]{1,0:T(1,128)} %cell.1, s32[1,512]{1,0:T(1,128)} %live.1, s32[8,1,512]{2,1,0:T(1,128)} %index.1, f32[8,1,512]{2,1,0:T(1,128)} %weight.1, f32[3,1,512]{2,1,0:T(1,128)} %direct.1, ...), custom_call_target="tpu_custom_call" | custom-call | tf_op jit(solution)/shard_map/pallas_call | solution.py:277
  18.8 0.0 copy-start
  18.8 1.5 %copy.12 = f32[3,8,8,128]{3,2,1,0:T(8,128)} copy(f32[3,8,8,128]{3,2,1,0:T(8,128)} %get-tuple-element.8) | data formatting | bytes 196608
  20.3 0.0 copy-done
  20.3 0.6 %copy.13 = f32[128,3]{0,1:T(4,128)} copy(f32[128,3]{0,1:T(4,128)S(1)} %bitcast.1) | data formatting | bytes 3072
Async XLA Ops:
  18.8 1.6 %copy-start = (f32[3,128]{1,0:T(4,128)S(1)}, f32[3,128]{1,0:T(4,128)}, u32[]{:S(2)}) copy-start(f32[3,128]{1,0:T(4,128)} %get-tuple-element.5) | copy-start | bytes 4612

commit v2 on v1

--- a/solution.py
+++ b/solution.py
@@ -30,9 +30,9 @@
     n_axial, n_span,
     stiff, rhs, cell, live, index, weight, direct, metric,
     adj_out, grad_out,
-    s_ext, r_ext, inv_ref, v_ref, p_ref, q_ref, own_v,
+    s_ext, r_ext, inv_ref, v_ref, p_ref, q_ref,
     cell_v, live_v, index_v, weight_v, direct_v, metric_v,
-    zhot, lohot, mw, send_g, recv_g, grad_v,
+    zhot, lohot, mw, send_g, recv_g,
     halo_send, halo_recv, g_send, g_recv, local_sem,
 ):
     u = lax.axis_index("axial")
@@ -95,6 +95,8 @@
     def span_of(pos, size):
         return 1 + (pos > 0).astype(jnp.int32) + (pos < size - 1).astype(jnp.int32)
 
+    loads[0].wait()
+    loads[1].wait()
     pl.semaphore_wait(barrier, span_of(u, n_axial) * span_of(t, n_span) + 4)
 
     def halo(k):
@@ -102,10 +104,10 @@
 
         def xs(width):
             if dx == 1:
-                return pl.ds(8 - width, width), pl.ds(4 - width, width)
+                return pl.ds(12 - width, width), pl.ds(4 - width, width)
             if dx == -1:
-                return pl.ds(0, width), pl.ds(12, width)
-            return pl.ds(0, 8), pl.ds(4, 8)
+                return pl.ds(4, width), pl.ds(12, width)
+            return pl.ds(4, 8), pl.ds(4, 8)
 
         ysrc, ydst = {1: (pl.ds(4, 4), pl.ds(12, 4)), -1: (pl.ds(0, 4), pl.ds(8, 4)), 0: (pl.ds(0, 8), pl.ds(0, 8))}[dy]
         sx, sxd = xs(4)
@@ -113,10 +115,10 @@
         target = (u + dx, t + dy)
         return (
             pltpu.make_async_remote_copy(
-                stiff.at[sx, ysrc], s_ext.at[sxd, ydst], halo_send.at[k, 0], halo_recv.at[k, 0],
+                s_ext.at[sx, ysrc], s_ext.at[sxd, ydst], halo_send.at[k, 0], halo_recv.at[k, 0],
                 device_id=target, device_id_type=MESH),
             pltpu.make_async_remote_copy(
-                rhs.at[:, rx, ysrc], r_ext.at[:, rxd, ydst], halo_send.at[k, 1], halo_recv.at[k, 1],
+                r_ext.at[:, rx, ysrc], r_ext.at[:, rxd, ydst], halo_send.at[k, 1], halo_recv.at[k, 1],
                 device_id=target, device_id_type=MESH),
         )
 
@@ -146,8 +148,6 @@
         mw[e] = jnp.where(
             lax.broadcasted_iota(jnp.int32, (8, slots), 0) == hi, weight_v[e], 0.0
         )
-    loads[0].wait()
-    loads[1].wait()
 
     for k, (dx, dy) in enumerate(DIRS):
         @pl.when(exists(-dx, -dy))
@@ -209,13 +209,10 @@
                 if sweep < SWEEPS - 1:
                     v_ref[i, mid] = new
                 else:
-                    own_v[i, c - 4:c - 4 + n] = new[:, 0:8]
-
-    out = pltpu.make_async_copy(own_v, adj_out, local_sem.at[0])
-    out.start()
-
-    rows = own_v.shape[1] * own_v.shape[2]
-    flat = own_v[...].reshape(3 * rows, 128)
+                    adj_out[i, c - 4:c - 4 + n] = new[:, 0:8]
+
+    rows = adj_out.shape[1] * adj_out.shape[2]
+    flat = adj_out[...].reshape(3 * rows, 128)
     top = flat.astype(jnp.bfloat16)
     rest = (flat - top.astype(jnp.float32)).astype(jnp.bfloat16)
     at = jnp.dot(top, zhot[...], preferred_element_type=jnp.float32)
@@ -257,13 +254,20 @@
     for h, copy in sends.items():
         copy.wait_recv()
         acc = acc + recv_g[h, 0:3]
-    grad_v[...] = acc
-    final = pltpu.make_async_copy(grad_v, grad_out, local_sem.at[1])
-    final.start()
+    grad_out[...] = acc
     for copy in sends.values():
         copy.wait_send()
-    out.wait()
-    final.wait()
+
+
+def write(adj, grad, adj_hbm, grad_hbm, sem):
+    copies = [
+        pltpu.make_async_copy(adj, adj_hbm, sem.at[0]),
+        pltpu.make_async_copy(grad, grad_hbm, sem.at[1]),
+    ]
+    for copy in copies:
+        copy.start()
+    for copy in copies:
+        copy.wait()
 
 
 def local(stiffness, adjoint_rhs, surf_cell, surf_live, ffd_index, ffd_weight, surf_direct, surf_metric):
@@ -277,11 +281,11 @@
     adjoint, grad = pl.pallas_call(
         functools.partial(kernel, n_axial, n_span),
         out_shape=(
-            jax.ShapeDtypeStruct(adjoint_rhs.shape, f32),
-            jax.ShapeDtypeStruct((3, lows), f32),
+            pltpu.VMEM(adjoint_rhs.shape, f32),
+            pltpu.VMEM((3, lows), f32),
         ),
         in_specs=[any_spec] * 8,
-        out_specs=(any_spec, any_spec),
+        out_specs=(pl.BlockSpec(memory_space=pltpu.VMEM),) * 2,
         scratch_shapes=[
             pltpu.VMEM((16, 16, 128), f32),
             pltpu.VMEM((3, 16, 16, 128), f32),
@@ -289,7 +293,6 @@
             pltpu.VMEM((3, 16, 16, 128), f32),
             pltpu.VMEM((3, 16, 16, 128), f32),
             pltpu.VMEM((6, 16, 16, 128), f32),
-            pltpu.VMEM(adjoint_rhs.shape, f32),
             pltpu.VMEM(surf_cell.shape, i32),
             pltpu.VMEM(surf_live.shape, i32),
             pltpu.VMEM(ffd_index.shape, i32),
@@ -301,7 +304,6 @@
             pltpu.VMEM((8, 8, slots), f32),
             pltpu.VMEM((6, 8, lows), f32),
             pltpu.VMEM((6, 8, lows), f32),
-            pltpu.VMEM((3, lows), f32),
             dma((8, 2)),
             dma((8, 2)),
             dma((6,)),
@@ -310,6 +312,17 @@
         ],
         compiler_params=pltpu.CompilerParams(collective_id=0, has_side_effects=True),
     )(stiffness, adjoint_rhs, surf_cell, surf_live, ffd_index, ffd_weight, surf_direct, surf_metric)
+    vmem_spec = pl.BlockSpec(memory_space=pltpu.VMEM)
+    adjoint, grad = pl.pallas_call(
+        write,
+        out_shape=(
+            jax.ShapeDtypeStruct(adjoint_rhs.shape, f32),
+            jax.ShapeDtypeStruct((3, lows), f32),
+        ),
+        in_specs=[vmem_spec] * 2,
+        out_specs=(any_spec, any_spec),
+        scratch_shapes=[dma((2,))],
+    )(*(pltpu.with_memory_space_constraint(a, pltpu.VMEM) for a in (adjoint, grad)))
     return adjoint, grad[:, :owned].T
 
 

time: 21 us -> 18.8 us (0.90)
  local copies, waits for them, and re-layouts: 2.12 us -> 0 us
    unnamed x4 -> x0, local copies, waits for them, and re-layouts: 2.12 us -> none
    pallas_call x1 -> x2, Pallas kernels: 18.1 us -> 18 us  [the longest x1 17.3 us: local(): pl.pallas_call(functools.partial(kernel, n_axial, n_span), out_shape=(plt...]
where the time goes in v2:
time: 18.8 us; the launch traced here: 18.6 us
  Pallas kernels  18 us (96%)
  between operations  0.64 us (3%)
    pallas_call x1, Pallas kernels, local(): pl.pallas_call(functools.partial(kernel, n_axial, n_span), out_shape=(plt...  17.3 us
    pallas_call x1, Pallas kernels, local(): pl.pallas_call(write, out_shape=(jax.ShapeDtypeStruct(adjoint_rhs.shape,...  0.66 us

profile of v2, /device:TPU:0, one launch (start us, length us, event | category | flops | bytes accessed | tf_op | source)
XLA Modules:
  0.0 18.6 jit_solution(2998159248289275313)
XLA Ops:
  0.6 17.3 %shard_map.95 = (f32[3,8,8,128]{3,2,1,0:T(8,128)S(1)}, f32[3,128]{1,0:T(4,128)S(1)}) custom-call(f32[8,8,128]{2,1,0:T(8,128)} %stiff.1, f32[3,8,8,128]{3,2,1,0:T(8,128)} %rhs.1, s32[1,512]{1,0:T(1,128)} %cell.1, s32[1,512]{1,0:T(1,128)} %live.1, s32[8,1,512]{2,1,0:T(1,128)} %index.1, f32[8,1,512]{2,1,0:T(1,128)} %weight.1, f32[3,1,512]{2,1,0:T(1,128)} %direct.1, ...), custom_call_target="tpu_custom_call" | custom-call | tf_op jit(solution)/shard_map/pallas_call | solution.py:281
  18.0 0.7 %shard_map.96 = (f32[3,8,8,128]{3,2,1,0:T(8,128)}, f32[3,128]{1,0:T(4,128)}) custom-call(f32[3,8,8,128]{3,2,1,0:T(8,128)S(1)} %get-tuple-element.6.adj, f32[3,128]{1,0:T(4,128)S(1)} %get-tuple-element.7.grad), custom_call_target="tpu_custom_call" | custom-call | tf_op jit(solution)/shard_map/pallas_call | solution.py:316

commit v3 on v2

--- a/solution.py
+++ b/solution.py
@@ -11,7 +11,7 @@
 NFFD = 4096
 CHUNK = 2
 MESH = pl.DeviceIdType.MESH
-DIRS = [(dx, dy) for dx in (-1, 0, 1) for dy in (-1, 0, 1) if (dx, dy) != (0, 0)]
+DIRS = [(0, 1), (0, -1), (1, 1), (1, -1), (-1, 1), (-1, -1), (1, 0), (-1, 0)]
 
 
 def yshift(a, step):
@@ -52,20 +52,8 @@
         pltpu.make_async_copy(direct, direct_v, local_sem.at[6]),
         pltpu.make_async_copy(metric, metric_v, local_sem.at[7]),
     ]
-    for load in loads[2:]:
+    for load in loads:
         load.start()
-
-    zero = jnp.zeros((8, 8, 128), jnp.float32)
-    zero4 = jnp.zeros((4, 16, 128), jnp.float32)
-    s_ext[0:4] = zero4
-    s_ext[12:16] = zero4
-    s_ext[4:12, 8:16] = zero
-    for i in range(3):
-        r_ext[i, 0:4] = zero4
-        r_ext[i, 12:16] = zero4
-        r_ext[i, 4:12, 8:16] = zero
-    loads[0].start()
-    loads[1].start()
 
     def owner(h):
         base = f + (count - 1) + h if h < 3 else f + (count - 1) + count // 2 + (h - 3)
@@ -86,12 +74,26 @@
         return ok
 
     barrier = pltpu.get_barrier_semaphore()
+    for h in (0, 2, 3, 4, 5):
+        pl.semaphore_signal(barrier, inc=1, device_id=sender(h), device_id_type=MESH)
     for dx, dy in DIRS:
         @pl.when(exists(dx, dy))
         def _(dx=dx, dy=dy):
             pl.semaphore_signal(barrier, inc=1, device_id=(u + dx, t + dy), device_id_type=MESH)
-    for h in (0, 2, 3, 4, 5):
-        pl.semaphore_signal(barrier, inc=1, device_id=sender(h), device_id_type=MESH)
+    def region(dx, dy):
+        xs = {0: slice(4, 12), 1: slice(12, 16), -1: slice(0, 4)}[dx]
+        ys = {0: slice(0, 8), 1: slice(8, 12), -1: slice(12, 16)}[dy]
+        return xs, ys
+
+    for dx, dy in DIRS:
+        @pl.when(jnp.logical_not(exists(dx, dy)))
+        def _(dx=dx, dy=dy):
+            xs, ys = region(dx, dy)
+            zero = jnp.zeros((xs.stop - xs.start, ys.stop - ys.start, 128), jnp.float32)
+            s_ext[xs, ys] = zero
+            for i in range(3):
+                r_ext[i, xs, ys] = zero
+
     def span_of(pos, size):
         return 1 + (pos > 0).astype(jnp.int32) + (pos < size - 1).astype(jnp.int32)
 
@@ -109,16 +111,24 @@
                 return pl.ds(4, width), pl.ds(12, width)
             return pl.ds(4, 8), pl.ds(4, 8)
 
-        ysrc, ydst = {1: (pl.ds(4, 4), pl.ds(12, 4)), -1: (pl.ds(0, 4), pl.ds(8, 4)), 0: (pl.ds(0, 8), pl.ds(0, 8))}[dy]
+        def ys(width):
+            if dy == 1:
+                return pl.ds(8 - width, width), pl.ds(16 - width, width)
+            if dy == -1:
+                return pl.ds(0, width), pl.ds(8, width)
+            return pl.ds(0, 8), pl.ds(0, 8)
+
         sx, sxd = xs(4)
         rx, rxd = xs(3)
+        sy, syd = ys(4)
+        ry, ryd = ys(3)
         target = (u + dx, t + dy)
         return (
             pltpu.make_async_remote_copy(
-                s_ext.at[sx, ysrc], s_ext.at[sxd, ydst], halo_send.at[k, 0], halo_recv.at[k, 0],
+                s_ext.at[sx, sy], s_ext.at[sxd, syd], halo_send.at[k, 0], halo_recv.at[k, 0],
                 device_id=target, device_id_type=MESH),
             pltpu.make_async_remote_copy(
-                r_ext.at[:, rx, ysrc], r_ext.at[:, rxd, ydst], halo_send.at[k, 1], halo_recv.at[k, 1],
+                r_ext.at[:, rx, ry], r_ext.at[:, rxd, ryd], halo_send.at[k, 1], halo_recv.at[k, 1],
                 device_id=target, device_id_type=MESH),
         )
 

time: 18.8 us -> 17.8 us (0.947)
  Pallas kernels: 18 us -> 17 us
    pallas_call x1, Pallas kernels: 17.3 us -> 16.4 us  [local(): pl.pallas_call(functools.partial(kernel, n_axial, n_span), out_shape=(plt...]
where the time goes in v3:
time: 17.8 us; the launch traced here: 17.7 us
  Pallas kernels  17 us (96%)
  between operations  0.64 us (4%)
    pallas_call x1, Pallas kernels, local(): pl.pallas_call(functools.partial(kernel, n_axial, n_span), out_shape=(plt...  16.4 us
    pallas_call x1, Pallas kernels, local(): pl.pallas_call(write, out_shape=(jax.ShapeDtypeStruct(adjoint_rhs.shape,...  0.66 us

profile of v3, /device:TPU:0, one launch (start us, length us, event | category | flops | bytes accessed | tf_op | source)
XLA Modules:
  0.0 17.7 jit_solution(7907054137210395190)
XLA Ops:
  0.6 16.4 %shard_map.95 = (f32[3,8,8,128]{3,2,1,0:T(8,128)S(1)}, f32[3,128]{1,0:T(4,128)S(1)}) custom-call(f32[8,8,128]{2,1,0:T(8,128)} %stiff.1, f32[3,8,8,128]{3,2,1,0:T(8,128)} %rhs.1, s32[1,512]{1,0:T(1,128)} %cell.1, s32[1,512]{1,0:T(1,128)} %live.1, s32[8,1,512]{2,1,0:T(1,128)} %index.1, f32[8,1,512]{2,1,0:T(1,128)} %weight.1, f32[3,1,512]{2,1,0:T(1,128)} %direct.1, ...), custom_call_target="tpu_custom_call" | custom-call | tf_op jit(solution)/shard_map/pallas_call | solution.py:291
  17.0 0.7 %shard_map.96 = (f32[3,8,8,128]{3,2,1,0:T(8,128)}, f32[3,128]{1,0:T(4,128)}) custom-call(f32[3,8,8,128]{3,2,1,0:T(8,128)S(1)} %get-tuple-element.6.adj, f32[3,128]{1,0:T(4,128)S(1)} %get-tuple-element.7.grad), custom_call_target="tpu_custom_call" | custom-call | tf_op jit(solution)/shard_map/pallas_call | solution.py:326

commit v4 on v3

--- a/solution.py
+++ b/solution.py
@@ -132,11 +132,11 @@
                 device_id=target, device_id_type=MESH),
         )
 
-    for k, (dx, dy) in enumerate(DIRS):
-        @pl.when(exists(dx, dy))
-        def _(k=k):
-            for copy in halo(k):
-                copy.start()
+    for piece in range(2):
+        for k, (dx, dy) in enumerate(DIRS):
+            @pl.when(exists(dx, dy))
+            def _(k=k, piece=piece):
+                halo(k)[piece].start()
 
     for load in loads[2:]:
         load.wait()
@@ -159,11 +159,13 @@
             lax.broadcasted_iota(jnp.int32, (8, slots), 0) == hi, weight_v[e], 0.0
         )
 
-    for k, (dx, dy) in enumerate(DIRS):
-        @pl.when(exists(-dx, -dy))
-        def _(k=k):
-            for copy in halo(k):
-                copy.wait_recv()
+    def arrived(piece):
+        for k, (dx, dy) in enumerate(DIRS):
+            @pl.when(exists(-dx, -dy))
+            def _(k=k):
+                halo(k)[piece].wait_recv()
+
+    arrived(0)
 
     for c, n in chunks(0, 16):
         s = s_ext[c:c + n]
@@ -177,8 +179,10 @@
         inv = jnp.where(s_ext[c:c + n] > 0, 1.0 / diag, 0.0)
         inv_ref[c:c + n] = inv
         q_ref[5, c:c + n] = diag
+    arrived(1)
+    for c, n in chunks(1, 15):
         for i in range(3):
-            v_ref[i, c:c + n] = r_ext[i, c:c + n] * inv
+            v_ref[i, c:c + n] = r_ext[i, c:c + n] * inv_ref[c:c + n]
 
     for sweep in range(SWEEPS):
         lo, hi = 2 + sweep, 14 - sweep
@@ -251,7 +255,7 @@
         h: pltpu.make_async_remote_copy(
             send_g.at[h], recv_g.at[h], g_send.at[h], g_recv.at[h],
             device_id=owner(h), device_id_type=MESH)
-        for h in (0, 2, 3, 4, 5)
+        for h in (3, 5, 4, 0, 2)
     }
     for copy in sends.values():
         copy.start()

time: 17.8 us -> 17.8 us (level)
  no operation moved by 1% of the time
where the time goes in v4:
time: 17.8 us; the launch traced here: 17.7 us
  Pallas kernels  17 us (96%)
  between operations  0.64 us (4%)
    pallas_call x1, Pallas kernels, local(): pl.pallas_call(functools.partial(kernel, n_axial, n_span), out_shape=(plt...  16.3 us
    pallas_call x1, Pallas kernels, local(): pl.pallas_call(write, out_shape=(jax.ShapeDtypeStruct(adjoint_rhs.shape,...  0.66 us

profile of v4, /device:TPU:0, one launch (start us, length us, event | category | flops | bytes accessed | tf_op | source)
XLA Modules:
  0.0 17.7 jit_solution(3022843662848637657)
XLA Ops:
  0.6 16.3 %shard_map.95 = (f32[3,8,8,128]{3,2,1,0:T(8,128)S(1)}, f32[3,128]{1,0:T(4,128)S(1)}) custom-call(f32[8,8,128]{2,1,0:T(8,128)} %stiff.1, f32[3,8,8,128]{3,2,1,0:T(8,128)} %rhs.1, s32[1,512]{1,0:T(1,128)} %cell.1, s32[1,512]{1,0:T(1,128)} %live.1, s32[8,1,512]{2,1,0:T(1,128)} %index.1, f32[8,1,512]{2,1,0:T(1,128)} %weight.1, f32[3,1,512]{2,1,0:T(1,128)} %direct.1, ...), custom_call_target="tpu_custom_call" | custom-call | tf_op jit(solution)/shard_map/pallas_call | solution.py:295
  17.0 0.7 %shard_map.96 = (f32[3,8,8,128]{3,2,1,0:T(8,128)}, f32[3,128]{1,0:T(4,128)}) custom-call(f32[3,8,8,128]{3,2,1,0:T(8,128)S(1)} %get-tuple-element.6.adj, f32[3,128]{1,0:T(4,128)S(1)} %get-tuple-element.7.grad), custom_call_target="tpu_custom_call" | custom-call | tf_op jit(solution)/shard_map/pallas_call | solution.py:330
